TPU v7x, 512 devices: a whole 4x4x16 slice. The times are simulated.
512 devices in a mesh: seq: 32 (over x, y, core), heads: 4 (over z_lo), dp: 4 (over z_hi).
Axes of the slice: x: 4, y: 4, z: 16 (z_hi: 4, z_lo: 4; z = z_hi * 4 + z_lo), core: 2. Of those that a mesh axis runs over, the one named last changes fastest.
Arguments:
- activations: bfloat16 [16384, 8192], P(('dp', 'seq'), 'heads'), parts along dimension 0, may hold values from -6 to 6
- conv_taps: bfloat16 [4, 8192], P(None, 'heads'), may hold values from -3 to 3
- gate_in: bfloat16 [8192, 1024], P('heads', 'seq'), may hold values from -0.0625 to 0.0625
- gate_out: bfloat16 [1024, 8], replicated, may hold values from -0.59765625 to 0.59765625
- queries: bfloat16 [16384, 8192], P(('dp', 'seq'), 'heads'), parts along dimension 0, may hold values from -1000 to 1000, as said below
- key_vectors: bfloat16 [16384, 1024], P(('dp', 'seq'), 'heads'), parts along dimension 0, may hold values from -4 to 4, as said below
- value_vectors: bfloat16 [16384, 1024], P(('dp', 'seq'), 'heads'), parts along dimension 0, may hold values from -6 to 6
- segment_ids: int32 [16384], P('dp'), parts along dimension 0, may hold values from 0 to 3, never falling along the last dimension, each value on 1 to 2048 neighbouring positions
Outputs:
- attended: bfloat16 [16384, 8192], P(('dp', 'seq'), 'heads'), parts along dimension 0
- key_mass: bfloat16 [8, 16384], P('heads', ('dp', 'seq')), parts along dimension 1
There are 4 independent parts, one for each index of `dp`. A program takes and returns all parts, laid end to end along the dimension named above; an argument that names none is the same for every part. Nothing has to cross between parts.
Inputs may be any that keep to these rules, and one draw needn't show every extreme that they name: `queries`: finite. `key_vectors`: finite.
All inputs are finite; a program needn't handle non-finite values.
Results may differ from a plain program's by a relative error of at most 0.0056.
Values may be sent and summed in bfloat16 or wider, within the bound.
A program may use at most 64 MiB of HBM per device.

v0:
```python
import math
import jax
import jax.numpy as jnp
from jax import lax
from jax.sharding import PartitionSpec as P

QUERY_HEADS = 64
KV_HEADS = 8
HEAD_DIM = 128
NEG_FILL = -1e30


def from_behind(block, axis, distance):
    devices = range(lax.axis_size(axis))
    route = [(i - distance, i) for i in devices if i - distance in devices]
    return lax.ppermute(block, axis, route)


def partner(x, axis, distance):
    return lax.ppermute(x, axis, [(i, i ^ 1 << distance) for i in range(lax.axis_size(axis))])


def key_places(flat_index, shard_rows, seq_count):
    half_rows = shard_rows // 2
    owner_dev = flat_index // shard_rows
    within = flat_index % shard_rows
    block_index = jnp.where(within < half_rows, 2 * owner_dev, 2 * seq_count - 1 - 2 * owner_dev)
    return block_index * half_rows + within % half_rows


def block_scores(query_heads, key_block, bias_block, allowed, score_scale):
    scores = (
        jnp.einsum("tgeh,kgh->getk", query_heads, key_block, preferred_element_type=jnp.float32)
        * score_scale
    )
    scores = scores + jnp.transpose(bias_block.astype(jnp.float32))[:, None, None, :]
    return jnp.where(allowed[None, None], scores, NEG_FILL)


def per_device(
    activations, conv_taps, gate_in, gate_out, queries, key_vectors, value_vectors, segment_ids
):
    shard_rows = activations.shape[0]
    tap_count = conv_taps.shape[0]
    rim_rows = from_behind(activations[shard_rows - (tap_count - 1) :], "seq", 1)
    widened = jnp.concatenate([rim_rows, activations], 0).astype(jnp.float32)
    summed = jnp.zeros(activations.shape, jnp.float32)
    for shift_back in range(tap_count):
        start_row = tap_count - 1 - shift_back
        summed = (
            summed
            + conv_taps[shift_back].astype(jnp.float32)
            * widened[start_row : start_row + shard_rows]
        )
    mixed_rows = summed.astype(jnp.bfloat16)
    partial_hidden = jnp.dot(
        mixed_rows,
        lax.all_gather(gate_in, "seq", axis=1, tiled=True),
        preferred_element_type=jnp.float32,
    )
    kv_local = key_vectors.shape[1] // HEAD_DIM
    group_size = QUERY_HEADS // KV_HEADS
    head_rank = lax.axis_index("heads")
    hidden = jax.nn.silu(lax.psum(partial_hidden, "heads")).astype(jnp.bfloat16)
    logits = jnp.dot(hidden, gate_out, preferred_element_type=jnp.float32)
    retention = lax.dynamic_slice_in_dim(
        jax.nn.log_sigmoid(logits).astype(jnp.bfloat16), head_rank * kv_local, kv_local, 1
    )
    seq_count = lax.axis_size("seq")
    seq_rank = lax.axis_index("seq")
    half_rows = shard_rows // 2
    local_index = jnp.arange(shard_rows, dtype=jnp.int32)
    moved_half = (
        queries[half_rows:],
        key_vectors[half_rows:],
        value_vectors[half_rows:],
        retention[half_rows:],
    )
    for bit_number in range(seq_count.bit_length() - 1):
        moved_half = partner(
            (moved_half[0], moved_half[1], moved_half[2], moved_half[3]), "seq", bit_number
        )
    own_queries = jnp.concatenate([queries[:half_rows], moved_half[0]], 0)
    own_keys = jnp.concatenate([key_vectors[:half_rows], moved_half[1]], 0)
    own_values = jnp.concatenate([value_vectors[:half_rows], moved_half[2]], 0)
    own_bias = jnp.concatenate([retention[:half_rows], moved_half[3]], 0)
    query_places = jnp.where(
        local_index < half_rows,
        2 * seq_rank * half_rows + local_index,
        (2 * seq_count - 1 - 2 * seq_rank) * half_rows + local_index - half_rows,
    )
    query_segments = jnp.take(segment_ids, query_places)
    query_heads = own_queries.reshape(shard_rows, kv_local, group_size, HEAD_DIM)
    score_scale = 1.0 / math.sqrt(HEAD_DIM)

    def visibility(flat_index):
        places = key_places(flat_index, shard_rows, seq_count)
        key_segments = jnp.take(segment_ids, places)
        return (places[None, :] <= query_places[:, None]) & (
            key_segments[None, :] == query_segments[:, None]
        )

    initial = (
        jnp.full((kv_local, group_size, shard_rows), NEG_FILL, jnp.float32),
        jnp.zeros((kv_local, group_size, shard_rows), jnp.float32),
    )
    all_keys, all_values, all_bias = (
        lax.all_gather(own_keys, "seq", axis=0, tiled=True),
        lax.all_gather(own_values, "seq", axis=0, tiled=True),
        lax.all_gather(own_bias, "seq", axis=0, tiled=True),
    )
    piece_rows = all_keys.shape[0]
    stats_block_width = math.gcd(piece_rows, 512)

    def one_block(block_number, state_in):
        offset = block_number * stats_block_width
        key_block = lax.dynamic_slice_in_dim(all_keys, offset, stats_block_width, 0).reshape(
            stats_block_width, kv_local, HEAD_DIM
        )
        bias_block = lax.dynamic_slice_in_dim(all_bias, offset, stats_block_width, 0)
        allowed = visibility(0 + offset + jnp.arange(stats_block_width, dtype=jnp.int32))

        def update(state_old):
            peak_old, mass_old = state_old
            masked = block_scores(query_heads, key_block, bias_block, allowed, score_scale)
            peak_new = jnp.maximum(peak_old, jnp.max(masked, axis=3))
            exponent = jnp.where(allowed[None, None], jnp.exp(masked - peak_new[..., None]), 0.0)
            return (peak_new, mass_old * jnp.exp(peak_old - peak_new) + jnp.sum(exponent, axis=3))

        def keep_state(state_old):
            return state_old

        return lax.cond(jnp.any(allowed), update, keep_state, state_in)

    row_peak, total_mass = lax.fori_loop(0, piece_rows // stats_block_width, one_block, initial)
    total_keys = all_keys.shape[0]
    block_width = math.gcd(total_keys, 512)
    block_count = total_keys // block_width
    key_blocks = all_keys.reshape(block_count, block_width, kv_local, HEAD_DIM)
    value_blocks = all_values.reshape(block_count, block_width, kv_local, HEAD_DIM)
    bias_blocks = all_bias.reshape(block_count, block_width, kv_local)

    def second_pass(accumulated, block_items):
        block_number, key_block, value_block, bias_block = block_items
        allowed = visibility(block_number * block_width + jnp.arange(block_width, dtype=jnp.int32))

        def attend(accum_in):
            masked = block_scores(query_heads, key_block, bias_block, allowed, score_scale)
            weights = (
                jnp.where(allowed[None, None], jnp.exp(masked - row_peak[..., None]), 0.0)
                / total_mass[..., None]
            )
            accum_out = accum_in + jnp.einsum(
                "getk,kgh->tgeh",
                weights.astype(jnp.bfloat16),
                value_block,
                preferred_element_type=jnp.float32,
            )
            return (accum_out, jnp.transpose(jnp.sum(weights, axis=(1, 2))) / group_size)

        def skip_block(accum_in):
            return (accum_in, jnp.zeros((block_width, kv_local), jnp.float32))

        return lax.cond(jnp.any(allowed), attend, skip_block, accumulated)

    accumulated, mass_blocks = lax.scan(
        second_pass,
        jnp.zeros((shard_rows, kv_local, group_size, HEAD_DIM), jnp.float32),
        (jnp.arange(block_count, dtype=jnp.int32), key_blocks, value_blocks, bias_blocks),
    )
    key_term = mass_blocks.reshape(total_keys, kv_local)
    key_mass = lax.psum_scatter(key_term, "seq", scatter_dimension=0, tiled=True).astype(
        jnp.bfloat16
    )
    attended = accumulated.reshape(shard_rows, kv_local * group_size * HEAD_DIM).astype(
        jnp.bfloat16
    )
    returned = (attended[half_rows:], key_mass[half_rows:])
    for bit_number in range(seq_count.bit_length() - 1):
        returned = partner((returned[0], returned[1]), "seq", bit_number)
    attended = jnp.concatenate([attended[:half_rows], returned[0]], 0)
    key_mass = jnp.concatenate([key_mass[:half_rows], returned[1]], 0)
    return (attended, jnp.transpose(key_mass))


def solution(mesh):
    return jax.shard_map(
        per_device,
        mesh=mesh,
        in_specs=(
            P(("dp", "seq"), "heads"),
            P(None, "heads"),
            P("heads", "seq"),
            P(),
            P(("dp", "seq"), "heads"),
            P(("dp", "seq"), "heads"),
            P(("dp", "seq"), "heads"),
            P("dp"),
        ),
        out_specs=(P(("dp", "seq"), "heads"), P("heads", ("dp", "seq"))),
        check_vma=False,
    )
```

profile of v0, /device:TPU:32, one launch (start us, length us, event | category | flops | bytes accessed | tf_op | source)
XLA Modules:
  0.0 626.7 jit_solution(121066509790797617)
XLA Ops:
  12.6 64.0 %all-gather.6.cloned.1.call-done = bf16[2048,1024]{0,1:T(8,128)(2,1)} async-done(((bf16[2048,32]{0,1:T(8,128)(2,1)}), bf16[2048,1024]{0,1:T(8,128)(2,1)}) %all-gather.6.cloned.1.call-update) | async-done | bytes 4194320 | tf_op jit(solution)/shard_map/all_gather | solution.py:58
  76.6 4.7 fusion.39
  84.6 3.1 collective-permute-start.1
  90.8 4.0 collective-permute-start.2
  94.8 3.7 collective-permute-done.2
  104.6 4.1 collective-permute-start.4
  108.8 3.5 collective-permute-done.4
  116.2 3.1 collective-permute-start.17
  122.0 4.0 collective-permute-start.18
  126.0 3.3 collective-permute-done.18
  129.3 3.1 collective-permute-start.19
  135.1 4.1 collective-permute-start.20
  139.1 3.2 collective-permute-done.20
  147.2 3.1 collective-permute-start.6
  150.3 12.8 %collective-permute-done.6 = bf16[64,2048]{0,1:T(8,128)(2,1)S(1)} collective-permute-done((bf16[64,2048]{0,1:T(8,128)(2,1)S(1)}, bf16[64,2048]{0,1:T(8,128)(2,1)S(1)}, u32[]{:S(2)}, u32[]{:S(2)}) %collective-permute-start.6) | collective-permute-done | bytes 262176 | tf_op jit(solution)/shard_map/ppermute | solution.py:20
  163.1 4.0 collective-permute-start.7
  167.1 13.2 %collective-permute-done.7 = bf16[64,2048]{0,1:T(8,128)(2,1)S(1)} collective-permute-done((bf16[64,2048]{0,1:T(8,128)(2,1)S(1)}, bf16[64,2048]{0,1:T(8,128)(2,1)S(1)}, u32[]{:S(2)}, u32[]{:S(2)}) %collective-permute-start.7) | collective-permute-done | bytes 262176 | tf_op jit(solution)/shard_map/ppermute | solution.py:20
  180.3 3.1 collective-permute-start.8
  183.4 11.0 %collective-permute-done.8 = bf16[64,2048]{0,1:T(8,128)(2,1)S(1)} collective-permute-done((bf16[64,2048]{0,1:T(8,128)(2,1)S(1)}, bf16[64,2048]{0,1:T(8,128)(2,1)S(1)}, u32[]{:S(2)}, u32[]{:S(2)}) %collective-permute-start.8) | collective-permute-done | bytes 262176 | tf_op jit(solution)/shard_map/ppermute | solution.py:20
  194.4 4.4 collective-permute-start.9
  208.8 3.5 collective-permute-start.13
  221.4 3.8 collective-permute-start.15
  228.3 49.2 %all-gather.8.cloned.1.call-done = bf16[4096,256]{1,0:T(8,128)(2,1)} async-done(((bf16[128,256]{1,0:T(8,128)(2,1)}), bf16[4096,256]{1,0:T(8,128)(2,1)}) %all-gather.8.cloned.1.call-update) | async-done | bytes 2097168 | tf_op jit(solution)/shard_map/all_gather | solution.py:109
  281.8 20.7 %all_gather.14 = bf16[4096,2]{0,1:T(2,128)(2,1)S(1)} all-gather(bf16[128,2]{0,1:T(2,128)(2,1)S(1)} %pad_maximum_fusion.4), channel_id=1, replica_groups=mesh['seq'=32,'heads'=4,'dp'=4] {'seq'}, dimensions={0}, use_global_device_ids=true | all-gather | bytes 16896 | tf_op jit(solution)/shard_map/all_gather | solution.py:110
  302.5 59.6 %while.38 = (s32[]{:T(128)}, f32[2,8,128]{2,1,0:T(8,128)S(1)}, f32[2,8,128]{2,1,0:T(8,128)S(1)}, s32[4096]{0:T(1024)S(1)}, s32[128]{0:T(128)S(1)}, /*index=5*/bf...) while((s32[]{:T(128)}, f32[2,8,128]{2,1,0:T(8,128)S(1)}, ...), condition=%wide.region_7.9_spmd.clone, body=%wide.region_1.8_spmd.clone.sunk | while | flops 279233152 | bytes 10043169 | solution.py:135
  302.5 3.1 gather_fusion
  307.3 3.4 conditional.6
  310.8 3.1 gather_fusion
  315.6 3.4 conditional.6
  319.1 3.1 gather_fusion
  323.9 3.4 conditional.6
  327.4 3.1 gather_fusion
  332.3 3.1 gather_fusion
  337.2 3.1 gather_fusion
  342.0 3.4 conditional.6
  345.5 3.1 gather_fusion
  350.3 3.4 conditional.6
  353.8 3.1 gather_fusion
  358.6 3.4 conditional.6
  362.2 75.0 %while.39 = (s32[]{:T(128)}, f32[128,2,8,128]{3,0,2,1:T(8,128)S(1)}, f32[8,512,2]{1,2,0:T(2,128)S(1)}, s32[8]{0:T(128)S(1)}, s32[4096]{0:T(1024)S(1)}, /*index=5...) while((s32[]{:T(128)}, ...), condition=%wide.region_13.15_spmd.clone, body=%wide.region_8.14_spmd.clone.sunk | while | flops 545829504 | bytes 7545635 | solution.py:166
  363.4 3.1 gather_fusion.1
  368.0 4.6 conditional.7
  374.0 3.1 gather_fusion.1
  378.6 4.6 conditional.7
  384.5 3.1 gather_fusion.1
  389.1 4.6 conditional.7
  395.0 3.1 gather_fusion.1
  401.0 3.1 gather_fusion.1
  406.9 3.1 gather_fusion.1
  411.5 4.6 conditional.7
  417.4 3.1 gather_fusion.1
  422.0 4.6 conditional.7
  428.0 3.1 gather_fusion.1
  432.6 4.6 conditional.7
  443.8 7.6 %collective-permute-done.22 = bf16[64,2048]{1,0:T(8,128)(2,1)S(1)} collective-permute-done((bf16[64,2048]{1,0:T(8,128)(2,1)S(1)}, bf16[64,2048]{1,0:T(8,128)(2,1)S(1)}, u32[]{:S(2)}, u32[]{:S(2)}) %collective-permute-start.22) | collective-permute-done | bytes 262176 | tf_op jit(solution)/shard_map/ppermute | solution.py:20
  451.5 4.3 collective-permute-start.23
  455.7 6.8 %collective-permute-done.23 = bf16[64,2048]{1,0:T(8,128)(2,1)S(1)} collective-permute-done((bf16[64,2048]{1,0:T(8,128)(2,1)S(1)}, bf16[64,2048]{1,0:T(8,128)(2,1)S(1)}, u32[]{:S(2)}, u32[]{:S(2)}) %collective-permute-start.23) | collective-permute-done | bytes 262176 | tf_op jit(solution)/shard_map/ppermute | solution.py:20
  462.5 18.0 %collective-permute-start.24 = (bf16[64,2048]{1,0:T(8,128)(2,1)S(1)}, bf16[64,2048]{1,0:T(8,128)(2,1)S(1)}, u32[]{:S(2)}, u32[]{:S(2)}) collective-permute-start(bf16[64,2048]{1,0:T(8,128)(2,1)S(1)} %collective-permute-done.23), channel_id=1, source_target_pairs={{0,128},{16,144},{32,160},{48,176},{64,192},{80,208},{96,224},{112... | collective-permute-start | bytes 786440 | tf_op jit(solution)/shard_map/ppermute | solution.py:20
  482.6 102.7 %reduce-scatter.4.cloned.1.call-done = f32[128,2]{1,0:T(8,128)} async-done(((f32[4096,2]{1,0:T(8,128)}), f32[128,2]{1,0:T(8,128)}) %reduce-scatter.4.cloned.1.call-update) | async-done | bytes 1040
  586.2 4.6 collective-permute-start.25
  595.8 3.5 collective-permute-done.27
  599.4 3.4 collective-permute-start.28
  602.7 3.6 collective-permute-done.28
  614.8 3.9 collective-permute-done.30
  (265 shorter events, 149.7 us)
Async XLA Ops:
  7.2 191.7 %copy-start = (bf16[1024,8]{0,1:T(8,128)(2,1)S(1)}, bf16[1024,8]{0,1:T(8,128)(2,1)}, u32[]{:S(2)}) copy-start(bf16[1024,8]{0,1:T(8,128)(2,1)} %param.21) | copy-start | bytes 49156
  7.2 69.4 %all-gather.6.cloned.1.call-start = ((), (), s32[]{:S(2)}) async-start(), calls=%async_computation.2 | async-start | bytes 4325376 | tf_op jit(solution)/shard_map/all_gather | solution.py:58
  7.9 190.9 %all-reduce.2.cloned.1.call-start = ((), (), s32[]{:S(2)}) async-start(), calls=%async_computation.3 | async-start | bytes 1048576 | tf_op jit(solution)/shard_map/psum | solution.py:64
  8.7 2.6 collective-permute-start.10
  76.6 4.8 copy-start.3
  76.6 36.5 %copy-start.4 = (bf16[128,256]{1,0:T(8,128)(2,1)S(1)}, bf16[128,256]{1,0:T(8,128)(2,1)}, u32[]{:S(2)}) copy-start(bf16[128,256]{1,0:T(8,128)(2,1)} %param.24) | copy-start | bytes 196612
  76.6 66.5 %copy-start.2 = (bf16[128,2048]{1,0:T(8,128)(2,1)S(1)}, bf16[128,2048]{1,0:T(8,128)(2,1)}, u32[]{:S(2)}) copy-start(bf16[128,2048]{1,0:T(8,128)(2,1)} %param.22) | copy-start | bytes 1572868
  81.3 120.9 %copy-start.1 = (s32[4096]{0:T(1024)S(1)}, s32[4096]{0:T(1024)}, u32[]{:S(2)}) copy-start(s32[4096]{0:T(1024)} %param.25) | copy-start | bytes 49156
  81.3 137.6 %all-gather.4.cloned.1.call-start = ((), (), s32[]{:S(2)}) async-start(), calls=%async_computation.1 | async-start | bytes 2162688 | tf_op jit(solution)/shard_map/all_gather | solution.py:108
  81.5 3.1 collective-permute-start
  84.6 6.1 collective-permute-start.1
  90.8 7.7 %collective-permute-start.2 = (bf16[64,256]{0,1:T(8,128)(2,1)S(1)}, bf16[64,256]{0,1:T(8,128)(2,1)S(1)}, u32[]{:S(2)}, u32[]{:S(2)}) collective-permute-start(bf16[64,256]{0,1:T(8,128)(2,1)S(1)} %collective-permute-done.1), channel_id=1, source_target_pairs={{0,64},{16,80},{32,96},{48,112},{64,0},{80,16},{96,32},{112,48},{1... | collective-permute-start | bytes 98312 | tf_op jit(solution)/shard_map/ppermute | solution.py:20
  98.4 6.1 collective-permute-start.3
  104.6 7.7 %collective-permute-start.4 = (bf16[64,256]{0,1:T(8,128)(2,1)S(1)}, bf16[64,256]{0,1:T(8,128)(2,1)S(1)}, u32[]{:S(2)}, u32[]{:S(2)}) collective-permute-start(bf16[64,256]{0,1:T(8,128)(2,1)S(1)} %collective-permute-done.3), channel_id=1, source_target_pairs={{0,256},{16,272},{32,288},{48,304},{64,320},{80,336},{96,352},{112... | collective-permute-start | bytes 98312 | tf_op jit(solution)/shard_map/ppermute | solution.py:20
  113.0 164.4 %all-gather.8.cloned.1.call-start = ((), (), s32[]{:S(2)}) async-start(), calls=%async_computation.4 | async-start | bytes 2162688 | tf_op jit(solution)/shard_map/all_gather | solution.py:109
  113.1 3.1 collective-permute-start.16
  116.2 5.8 collective-permute-start.17
  122.0 7.3 %collective-permute-start.18 = (bf16[64,256]{1,0:T(8,128)(2,1)S(1)}, bf16[64,256]{1,0:T(8,128)(2,1)S(1)}, u32[]{:S(2)}, u32[]{:S(2)}) collective-permute-start(bf16[64,256]{1,0:T(8,128)(2,1)S(1)} %collective-permute-done.17), channel_id=1, source_target_pairs={{0,64},{16,80},{32,96},{48,112},{64,0},{80,16},{96,32},{112,48},{1... | collective-permute-start | bytes 98312 | tf_op jit(solution)/shard_map/ppermute | solution.py:20
  129.3 5.8 collective-permute-start.19
  135.1 7.3 %collective-permute-start.20 = (bf16[64,256]{1,0:T(8,128)(2,1)S(1)}, bf16[64,256]{1,0:T(8,128)(2,1)S(1)}, u32[]{:S(2)}, u32[]{:S(2)}) collective-permute-start(bf16[64,256]{1,0:T(8,128)(2,1)S(1)} %collective-permute-done.19), channel_id=1, source_target_pairs={{0,256},{16,272},{32,288},{48,304},{64,320},{80,336},{96,352},{112... | collective-permute-start | bytes 98312 | tf_op jit(solution)/shard_map/ppermute | solution.py:20
  143.0 442.3 %reduce-scatter.4.cloned.1.call-start = ((), (), s32[]{:S(2)}) async-start(), calls=%async_computation.5 | async-start | bytes 2162688
  143.4 3.8 collective-permute-start.5
  147.2 15.8 %collective-permute-start.6 = (bf16[64,2048]{0,1:T(8,128)(2,1)S(1)}, bf16[64,2048]{0,1:T(8,128)(2,1)S(1)}, u32[]{:S(2)}, u32[]{:S(2)}) collective-permute-start(bf16[64,2048]{0,1:T(8,128)(2,1)S(1)} %collective-permute-done.5), channel_id=1, source_target_pairs={{0,32},{16,48},{32,0},{48,16},{64,96},{80,112},{96,64},{112,80},{1... | collective-permute-start | bytes 786440 | tf_op jit(solution)/shard_map/ppermute | solution.py:20
  163.1 17.2 %collective-permute-start.7 = (bf16[64,2048]{0,1:T(8,128)(2,1)S(1)}, bf16[64,2048]{0,1:T(8,128)(2,1)S(1)}, u32[]{:S(2)}, u32[]{:S(2)}) collective-permute-start(bf16[64,2048]{0,1:T(8,128)(2,1)S(1)} %collective-permute-done.6), channel_id=1, source_target_pairs={{0,64},{16,80},{32,96},{48,112},{64,0},{80,16},{96,32},{112,48},{1... | collective-permute-start | bytes 786440 | tf_op jit(solution)/shard_map/ppermute | solution.py:20
  180.3 14.1 %collective-permute-start.8 = (bf16[64,2048]{0,1:T(8,128)(2,1)S(1)}, bf16[64,2048]{0,1:T(8,128)(2,1)S(1)}, u32[]{:S(2)}, u32[]{:S(2)}) collective-permute-start(bf16[64,2048]{0,1:T(8,128)(2,1)S(1)} %collective-permute-done.7), channel_id=1, source_target_pairs={{0,128},{16,144},{32,160},{48,176},{64,192},{80,208},{96,224},{112... | collective-permute-start | bytes 786440 | tf_op jit(solution)/shard_map/ppermute | solution.py:20
  194.4 19.0 %collective-permute-start.9 = (bf16[64,2048]{0,1:T(8,128)(2,1)S(1)}, bf16[64,2048]{0,1:T(8,128)(2,1)S(1)}, u32[]{:S(2)}, u32[]{:S(2)}) collective-permute-start(bf16[64,2048]{0,1:T(8,128)(2,1)S(1)} %collective-permute-done.8), channel_id=1, source_target_pairs={{0,256},{16,272},{32,288},{48,304},{64,320},{80,336},{96,352},{112... | collective-permute-start | bytes 786440 | tf_op jit(solution)/shard_map/ppermute | solution.py:20
  200.3 3.1 collective-permute-start.11
  203.4 5.5 collective-permute-start.12
  208.8 7.0 %collective-permute-start.13 = (bf16[64,2]{0,1:T(2,128)(2,1)S(1)}, bf16[64,2]{0,1:T(2,128)(2,1)S(1)}, u32[]{:S(2)}, u32[]{:S(2)}) collective-permute-start(bf16[64,2]{0,1:T(2,128)(2,1)S(1)} %collective-permute-done.12), channel_id=1, source_target_pairs={{0,64},{16,80},{32,96},{48,112},{64,0},{80,16},{96,32},{112,48},{1... | collective-permute-start | bytes 776 | tf_op jit(solution)/shard_map/ppermute | solution.py:20
  215.8 5.6 collective-permute-start.14
  221.4 60.3 %collective-permute-start.15 = (bf16[64,2]{0,1:T(2,128)(2,1)S(1)}, bf16[64,2]{0,1:T(2,128)(2,1)S(1)}, u32[]{:S(2)}, u32[]{:S(2)}) collective-permute-start(bf16[64,2]{0,1:T(2,128)(2,1)S(1)} %collective-permute-done.14), channel_id=1, source_target_pairs={{0,256},{16,272},{32,288},{48,304},{64,320},{80,336},{96,352},{112... | collective-permute-start | bytes 776 | tf_op jit(solution)/shard_map/ppermute | solution.py:20
  437.6 3.4 collective-permute-start.21
  441.0 10.4 %collective-permute-start.22 = (bf16[64,2048]{1,0:T(8,128)(2,1)S(1)}, bf16[64,2048]{1,0:T(8,128)(2,1)S(1)}, u32[]{:S(2)}, u32[]{:S(2)}) collective-permute-start(bf16[64,2048]{1,0:T(8,128)(2,1)S(1)} %collective-permute-done.21), channel_id=1, source_target_pairs={{0,32},{16,48},{32,0},{48,16},{64,96},{80,112},{96,64},{112,80},{1... | collective-permute-start | bytes 786440 | tf_op jit(solution)/shard_map/ppermute | solution.py:20
  451.5 11.1 %collective-permute-start.23 = (bf16[64,2048]{1,0:T(8,128)(2,1)S(1)}, bf16[64,2048]{1,0:T(8,128)(2,1)S(1)}, u32[]{:S(2)}, u32[]{:S(2)}) collective-permute-start(bf16[64,2048]{1,0:T(8,128)(2,1)S(1)} %collective-permute-done.22), channel_id=1, source_target_pairs={{0,64},{16,80},{32,96},{48,112},{64,0},{80,16},{96,32},{112,48},{1... | collective-permute-start | bytes 786440 | tf_op jit(solution)/shard_map/ppermute | solution.py:20
  462.5 123.7 %collective-permute-start.24 = (bf16[64,2048]{1,0:T(8,128)(2,1)S(1)}, bf16[64,2048]{1,0:T(8,128)(2,1)S(1)}, u32[]{:S(2)}, u32[]{:S(2)}) collective-permute-start(bf16[64,2048]{1,0:T(8,128)(2,1)S(1)} %collective-permute-done.23), channel_id=1, source_target_pairs={{0,128},{16,144},{32,160},{48,176},{64,192},{80,208},{96,224},{112... | collective-permute-start | bytes 786440 | tf_op jit(solution)/shard_map/ppermute | solution.py:20
  586.2 33.1 %collective-permute-start.25 = (bf16[64,2048]{1,0:T(8,128)(2,1)S(1)}, bf16[64,2048]{1,0:T(8,128)(2,1)S(1)}, u32[]{:S(2)}, u32[]{:S(2)}) collective-permute-start(bf16[64,2048]{1,0:T(8,128)(2,1)S(1)} %collective-permute-done.24), channel_id=1, source_target_pairs={{0,256},{16,272},{32,288},{48,304},{64,320},{80,336},{96,352},{112... | collective-permute-start | bytes 786440 | tf_op jit(solution)/shard_map/ppermute | solution.py:20
  590.9 3.0 collective-permute-start.26
  593.9 5.5 collective-permute-start.27
  599.4 7.0 %collective-permute-start.28 = (bf16[64,2]{0,1:T(2,128)(2,1)S(1)}, bf16[64,2]{0,1:T(2,128)(2,1)S(1)}, u32[]{:S(2)}, u32[]{:S(2)}) collective-permute-start(bf16[64,2]{0,1:T(2,128)(2,1)S(1)} %collective-permute-done.27), channel_id=1, source_target_pairs={{0,64},{16,80},{32,96},{48,112},{64,0},{80,16},{96,32},{112,48},{1... | collective-permute-start | bytes 776 | tf_op jit(solution)/shard_map/ppermute | solution.py:20
  606.3 5.5 collective-permute-start.29
  611.8 7.0 %collective-permute-start.30 = (bf16[64,2]{0,1:T(2,128)(2,1)S(1)}, bf16[64,2]{0,1:T(2,128)(2,1)S(1)}, u32[]{:S(2)}, u32[]{:S(2)}) collective-permute-start(bf16[64,2]{0,1:T(2,128)(2,1)S(1)} %collective-permute-done.29), channel_id=1, source_target_pairs={{0,256},{16,272},{32,288},{48,304},{64,320},{80,336},{96,352},{112... | collective-permute-start | bytes 776 | tf_op jit(solution)/shard_map/ppermute | solution.py:20
Sparse Core Ops, SparseCore 0:
  11.1 65.4 all-gather.5
  81.4 60.2 all-reduce.1
  144.7 69.4 all-gather.3
  217.2 60.1 all-gather.7
  482.7 102.5 reduce-scatter.3
where the time goes:
time: 629 us; the launch traced here: 627 us
  waiting for transfers between devices  319 us (51%)
  starting transfers between devices  110 us (17%)
  local copies, waits for them, and re-layouts  77.6 us (12%)
  matrix products  40.3 us (6%)
  other arithmetic  27.1 us (4%)
  blocking collectives  20.7 us (3%)
  loops' own time  17.6 us (3%)
  between operations  14.3 us (2%)
    ppermute x30, starting transfers between devices, partner(): lax.ppermute(x, axis, [(i, i ^ 1 << distance) for i in range(lax.axis_siz...  108 us
    unnamed x6, waiting for transfers between devices  103 us
    ppermute x30, waiting for transfers between devices, partner(): lax.ppermute(x, axis, [(i, i ^ 1 << distance) for i in range(lax.axis_siz...  103 us
    all_gather x1, waiting for transfers between devices, per_device(): lax.all_gather(gate_in, 'seq', axis=1, tiled=True)  64 us
    gather x16, local copies, waits for them, and re-layouts, visibility(): key_segments = jnp.take(segment_ids, places)  50.3 us
    all_gather x1, waiting for transfers between devices, per_device(): lax.all_gather(own_values, 'seq', axis=0, tiled=True)  49.2 us
    dot_general x12, matrix products, block_scores(): jnp.einsum('tgeh,kgh->getk', query_heads, key_block, preferred_element_ty...  24 us
    all_gather x1, blocking collectives, per_device(): lax.all_gather(own_bias, 'seq', axis=0, tiled=True)  20.7 us
  transfers between devices with their start and end apart: 36, of which 28 were waited for; matrix products, arithmetic and copies ran while one was open for 3% of the time, Pallas kernels for 0%

commit v1 on v0

--- a/solution.py
+++ b/solution.py
@@ -55,7 +55,9 @@
     mixed_rows = summed.astype(jnp.bfloat16)
     partial_hidden = jnp.dot(
         mixed_rows,
-        lax.all_gather(gate_in, "seq", axis=1, tiled=True),
+        jnp.concatenate(
+            lax.all_to_all(jnp.stack([gate_in] * lax.axis_size("seq")), "seq", 0, 0), axis=1
+        ),
         preferred_element_type=jnp.float32,
     )
     kv_local = key_vectors.shape[1] // HEAD_DIM

time: 629 us -> 595 us (0.946)
  waiting for transfers between devices: 319 us -> 280 us
    all_gather x1 -> x0, waiting for transfers between devices: 64 us -> none  [per_device(): lax.all_gather(gate_in, 'seq', axis=1, tiled=True)]
    all_to_all x0 -> x1, waiting for transfers between devices: none -> 49.3 us  [per_device(): lax.all_to_all(jnp.stack([gate_in] * lax.axis_size('seq')), 'seq', 0, 0)]
    all_gather x1, waiting for transfers between devices: 49.2 us -> 17.8 us  [per_device(): lax.all_gather(own_values, 'seq', axis=0, tiled=True)]
    all_to_all x0 -> x1, starting transfers between devices: none -> 7.58 us  [per_device(): lax.all_to_all(jnp.stack([gate_in] * lax.axis_size('seq')), 'seq', 0, 0)]
    ppermute x30, waiting for transfers between devices: 103 us -> 110 us  [partner(): lax.ppermute(x, axis, [(i, i ^ 1 << distance) for i in range(lax.axis_siz...]
    unnamed x6 -> x5, waiting for transfers between devices: 103 us -> 103 us
where the time goes in v1:
time: 595 us; the launch traced here: 593 us
  waiting for transfers between devices  280 us (47%)
  starting transfers between devices  114 us (19%)
  local copies, waits for them, and re-layouts  80.1 us (13%)
  matrix products  40.2 us (7%)
  other arithmetic  24.7 us (4%)
  blocking collectives  20.8 us (3%)
  loops' own time  17 us (3%)
  between operations  16.3 us (3%)
    ppermute x30, waiting for transfers between devices, partner(): lax.ppermute(x, axis, [(i, i ^ 1 << distance) for i in range(lax.axis_siz...  110 us
    ppermute x30, starting transfers between devices, partner(): lax.ppermute(x, axis, [(i, i ^ 1 << distance) for i in range(lax.axis_siz...  104 us
    unnamed x5, waiting for transfers between devices  103 us
    gather x16, local copies, waits for them, and re-layouts, visibility(): key_segments = jnp.take(segment_ids, places)  50.3 us
    all_to_all x1, waiting for transfers between devices, per_device(): lax.all_to_all(jnp.stack([gate_in] * lax.axis_size('seq')), 'seq', 0, 0)  49.3 us
    dot_general x12, matrix products, block_scores(): jnp.einsum('tgeh,kgh->getk', query_heads, key_block, preferred_element_ty...  23.9 us
    all_gather x1, blocking collectives, per_device(): lax.all_gather(own_bias, 'seq', axis=0, tiled=True)  20.8 us
    all_gather x1, waiting for transfers between devices, per_device(): lax.all_gather(own_values, 'seq', axis=0, tiled=True)  17.8 us
  transfers between devices with their start and end apart: 36, of which 28 were waited for; matrix products, arithmetic and copies ran while one was open for 3% of the time, Pallas kernels for 0%

profile of v1, /device:TPU:32, one launch (start us, length us, event | category | flops | bytes accessed | tf_op | source)
XLA Modules:
  0.0 593.1 jit_solution(15315571958458670738)
XLA Ops:
  8.0 3.4 stack.2
  11.5 7.6 %all-to-all-start = ((bf16[32,2048,32]{1,2,0:T(8,128)(2,1)}), bf16[32,2048,32]{1,2,0:T(8,128)(2,1)}, u32[]{:S(2)}, u32[]{:S(2)}) async-start(bf16[32,2048,32]{1,2,0:T(8,128)(2,1)} %stack.2), calls=%async_computation | async-start | bytes 8388608 | tf_op jit(solution)/shard_map/all_to_all | solution.py:59
  22.2 49.3 %all-to-all-done = bf16[32,2048,32]{1,2,0:T(8,128)(2,1)} async-done(((bf16[32,2048,32]{1,2,0:T(8,128)(2,1)}), bf16[32,2048,32]{1,2,0:T(8,128)(2,1)}, u32[]{:S(2)}, u32[]{:S(2)}) %all-to-all-start) | async-done | bytes 4194336 | tf_op jit(solution)/shard_map/all_to_all | solution.py:59
  71.5 4.7 fusion.39
  79.6 4.3 collective-permute-start.1
  89.2 4.8 collective-permute-done.2
  95.9 4.2 collective-permute-done.3
  103.0 4.7 collective-permute-done.4
  111.6 3.7 collective-permute-start.17
  117.4 3.5 collective-permute-start.18
  120.9 3.8 collective-permute-done.18
  126.7 3.8 collective-permute-done.19
  133.4 4.5 collective-permute-done.20
  142.7 3.8 collective-permute-start.6
  146.5 12.9 %collective-permute-done.6 = bf16[64,2048]{0,1:T(8,128)(2,1)S(1)} collective-permute-done((bf16[64,2048]{0,1:T(8,128)(2,1)S(1)}, bf16[64,2048]{0,1:T(8,128)(2,1)S(1)}, u32[]{:S(2)}, u32[]{:S(2)}) %collective-permute-start.6) | collective-permute-done | bytes 262176 | tf_op jit(solution)/shard_map/ppermute | solution.py:20
  162.1 14.9 %collective-permute-done.7 = bf16[64,2048]{0,1:T(8,128)(2,1)S(1)} collective-permute-done((bf16[64,2048]{0,1:T(8,128)(2,1)S(1)}, bf16[64,2048]{0,1:T(8,128)(2,1)S(1)}, u32[]{:S(2)}, u32[]{:S(2)}) %collective-permute-start.7) | collective-permute-done | bytes 262176 | tf_op jit(solution)/shard_map/ppermute | solution.py:20
  177.0 3.1 collective-permute-start.8
  180.1 11.6 %collective-permute-done.8 = bf16[64,2048]{0,1:T(8,128)(2,1)S(1)} collective-permute-done((bf16[64,2048]{0,1:T(8,128)(2,1)S(1)}, bf16[64,2048]{0,1:T(8,128)(2,1)S(1)}, u32[]{:S(2)}, u32[]{:S(2)}) %collective-permute-start.8) | collective-permute-done | bytes 262176 | tf_op jit(solution)/shard_map/ppermute | solution.py:20
  191.7 4.6 collective-permute-start.9
  203.1 3.2 collective-permute-done.12
  206.3 4.8 collective-permute-start.13
  219.1 3.9 collective-permute-start.15
  226.0 17.8 %all-gather.5.cloned.1.call-done = bf16[4096,256]{1,0:T(8,128)(2,1)} async-done(((bf16[128,256]{1,0:T(8,128)(2,1)}), bf16[4096,256]{1,0:T(8,128)(2,1)}) %all-gather.5.cloned.1.call-update) | async-done | bytes 2097168 | tf_op jit(solution)/shard_map/all_gather | solution.py:111
  248.3 20.8 %all_gather.10 = bf16[4096,2]{0,1:T(2,128)(2,1)S(1)} all-gather(bf16[128,2]{0,1:T(2,128)(2,1)S(1)} %pad_maximum_fusion.4), channel_id=1, replica_groups=mesh['seq'=32,'heads'=4,'dp'=4] {'seq'}, dimensions={0}, use_global_device_ids=true | all-gather | bytes 16896 | tf_op jit(solution)/shard_map/all_gather | solution.py:112
  269.0 58.5 %while.38 = (s32[]{:T(128)}, f32[2,8,128]{2,1,0:T(8,128)S(1)}, f32[2,8,128]{2,1,0:T(8,128)S(1)}, s32[4096]{0:T(1024)S(1)}, s32[128]{0:T(128)S(1)}, /*index=5*/bf...) while((s32[]{:T(128)}, f32[2,8,128]{2,1,0:T(8,128)S(1)}, ...), condition=%wide.region_7.9_spmd.clone, body=%wide.region_1.8_spmd.clone.sunk | while | flops 279233152 | bytes 10043169 | solution.py:137
  269.0 3.1 gather_fusion
  273.7 3.4 conditional.6
  277.2 3.1 gather_fusion
  281.9 3.4 conditional.6
  285.4 3.1 gather_fusion
  290.1 3.4 conditional.6
  293.5 3.1 gather_fusion
  298.3 3.1 gather_fusion
  303.0 3.1 gather_fusion
  307.7 3.4 conditional.6
  311.2 3.1 gather_fusion
  315.9 3.4 conditional.6
  319.4 3.1 gather_fusion
  324.0 3.4 conditional.6
  327.6 75.0 %while.39 = (s32[]{:T(128)}, f32[128,2,8,128]{3,0,2,1:T(8,128)S(1)}, f32[8,512,2]{1,2,0:T(2,128)S(1)}, s32[8]{0:T(128)S(1)}, s32[4096]{0:T(1024)S(1)}, /*index=5...) while((s32[]{:T(128)}, ...), condition=%wide.region_13.15_spmd.clone, body=%wide.region_8.14_spmd.clone.sunk | while | flops 545829504 | bytes 7545635 | solution.py:168
  328.9 3.1 gather_fusion.1
  333.5 4.6 conditional.7
  339.4 3.1 gather_fusion.1
  344.0 4.6 conditional.7
  349.9 3.1 gather_fusion.1
  354.5 4.6 conditional.7
  360.4 3.1 gather_fusion.1
  366.4 3.1 gather_fusion.1
  372.3 3.1 gather_fusion.1
  376.9 4.6 conditional.7
  382.8 3.1 gather_fusion.1
  387.5 4.6 conditional.7
  393.4 3.1 gather_fusion.1
  398.0 4.6 conditional.7
  409.2 7.6 %collective-permute-done.22 = bf16[64,2048]{1,0:T(8,128)(2,1)S(1)} collective-permute-done((bf16[64,2048]{1,0:T(8,128)(2,1)S(1)}, bf16[64,2048]{1,0:T(8,128)(2,1)S(1)}, u32[]{:S(2)}, u32[]{:S(2)}) %collective-permute-start.22) | collective-permute-done | bytes 262176 | tf_op jit(solution)/shard_map/ppermute | solution.py:20
  416.9 4.3 collective-permute-start.23
  421.1 6.8 %collective-permute-done.23 = bf16[64,2048]{1,0:T(8,128)(2,1)S(1)} collective-permute-done((bf16[64,2048]{1,0:T(8,128)(2,1)S(1)}, bf16[64,2048]{1,0:T(8,128)(2,1)S(1)}, u32[]{:S(2)}, u32[]{:S(2)}) %collective-permute-start.23) | collective-permute-done | bytes 262176 | tf_op jit(solution)/shard_map/ppermute | solution.py:20
  427.9 17.9 %collective-permute-start.24 = (bf16[64,2048]{1,0:T(8,128)(2,1)S(1)}, bf16[64,2048]{1,0:T(8,128)(2,1)S(1)}, u32[]{:S(2)}, u32[]{:S(2)}) collective-permute-start(bf16[64,2048]{1,0:T(8,128)(2,1)S(1)} %collective-permute-done.23), channel_id=1, source_target_pairs={{0,128},{16,144},{32,160},{48,176},{64,192},{80,208},{96,224},{112... | collective-permute-start | bytes 786440 | tf_op jit(solution)/shard_map/ppermute | solution.py:20
  447.9 102.7 %reduce-scatter.4.cloned.1.call-done = f32[128,2]{1,0:T(8,128)} async-done(((f32[4096,2]{1,0:T(8,128)}), f32[128,2]{1,0:T(8,128)}) %reduce-scatter.4.cloned.1.call-update) | async-done | bytes 1040
  551.5 4.6 collective-permute-start.25
  561.2 3.5 collective-permute-done.27
  564.7 3.4 collective-permute-start.28
  568.1 3.6 collective-permute-done.28
  580.1 3.9 collective-permute-done.30
  (269 shorter events, 147.7 us)
Async XLA Ops:
  8.0 188.3 %copy-start = (bf16[1024,8]{0,1:T(8,128)(2,1)S(1)}, bf16[1024,8]{0,1:T(8,128)(2,1)}, u32[]{:S(2)}) copy-start(bf16[1024,8]{0,1:T(8,128)(2,1)} %param.21) | copy-start | bytes 49156
  11.5 7.6 %copy-start.2 = (bf16[128,2048]{1,0:T(8,128)(2,1)S(1)}, bf16[128,2048]{1,0:T(8,128)(2,1)}, u32[]{:S(2)}) copy-start(bf16[128,2048]{1,0:T(8,128)(2,1)} %param.18) | copy-start | bytes 1572868
  11.5 9.8 %copy-start.6 = (bf16[4,2048]{1,0:T(4,128)(2,1)S(1)}, bf16[4,2048]{1,0:T(4,128)(2,1)}, u32[]{:S(2)}) copy-start(bf16[4,2048]{1,0:T(4,128)(2,1)} %param.19) | copy-start | bytes 49156
  11.5 60.0 %all-to-all-start = ((bf16[32,2048,32]{1,2,0:T(8,128)(2,1)}), bf16[32,2048,32]{1,2,0:T(8,128)(2,1)}, u32[]{:S(2)}, u32[]{:S(2)}) async-start(bf16[32,2048,32]{1,2,0:T(8,128)(2,1)} %stack.2), calls=%async_computation | async-start | bytes 8388608 | tf_op jit(solution)/shard_map/all_to_all | solution.py:59
  19.0 177.3 %all-reduce.2.cloned.1.call-start = ((), (), s32[]{:S(2)}) async-start(), calls=%async_computation.3 | async-start | bytes 1048576 | tf_op jit(solution)/shard_map/psum | solution.py:66
  19.1 2.9 collective-permute-start.10
  71.5 4.8 copy-start.4
  71.5 37.0 %copy-start.5 = (bf16[128,256]{1,0:T(8,128)(2,1)S(1)}, bf16[128,256]{1,0:T(8,128)(2,1)}, u32[]{:S(2)}) copy-start(bf16[128,256]{1,0:T(8,128)(2,1)} %param.24) | copy-start | bytes 196612
  71.5 67.0 %copy-start.3 = (bf16[128,2048]{1,0:T(8,128)(2,1)S(1)}, bf16[128,2048]{1,0:T(8,128)(2,1)}, u32[]{:S(2)}) copy-start(bf16[128,2048]{1,0:T(8,128)(2,1)} %param.22) | copy-start | bytes 1572868
  76.2 123.5 %copy-start.1 = (s32[4096]{0:T(1024)S(1)}, s32[4096]{0:T(1024)}, u32[]{:S(2)}) copy-start(s32[4096]{0:T(1024)} %param.25) | copy-start | bytes 49156
  76.2 140.4 %all-gather.3.cloned.1.call-start = ((), (), s32[]{:S(2)}) async-start(), calls=%async_computation.2 | async-start | bytes 2162688 | tf_op jit(solution)/shard_map/all_gather | solution.py:110
  76.4 3.1 collective-permute-start
  79.6 6.7 %collective-permute-start.1 = (bf16[64,256]{0,1:T(8,128)(2,1)S(1)}, bf16[64,256]{0,1:T(8,128)(2,1)S(1)}, u32[]{:S(2)}, u32[]{:S(2)}) collective-permute-start(bf16[64,256]{0,1:T(8,128)(2,1)S(1)} %collective-permute-done), channel_id=1, source_target_pairs={{0,32},{16,48},{32,0},{48,16},{64,96},{80,112},{96,64},{112,80},{1... | collective-permute-start | bytes 98312 | tf_op jit(solution)/shard_map/ppermute | solution.py:20
  86.3 7.7 %collective-permute-start.2 = (bf16[64,256]{0,1:T(8,128)(2,1)S(1)}, bf16[64,256]{0,1:T(8,128)(2,1)S(1)}, u32[]{:S(2)}, u32[]{:S(2)}) collective-permute-start(bf16[64,256]{0,1:T(8,128)(2,1)S(1)} %collective-permute-done.1), channel_id=1, source_target_pairs={{0,64},{16,80},{32,96},{48,112},{64,0},{80,16},{96,32},{112,48},{1... | collective-permute-start | bytes 98312 | tf_op jit(solution)/shard_map/ppermute | solution.py:20
  93.9 6.1 %collective-permute-start.3 = (bf16[64,256]{0,1:T(8,128)(2,1)S(1)}, bf16[64,256]{0,1:T(8,128)(2,1)S(1)}, u32[]{:S(2)}, u32[]{:S(2)}) collective-permute-start(bf16[64,256]{0,1:T(8,128)(2,1)S(1)} %collective-permute-done.2), channel_id=1, source_target_pairs={{0,128},{16,144},{32,160},{48,176},{64,192},{80,208},{96,224},{112... | collective-permute-start | bytes 98312 | tf_op jit(solution)/shard_map/ppermute | solution.py:20
  100.1 7.7 %collective-permute-start.4 = (bf16[64,256]{0,1:T(8,128)(2,1)S(1)}, bf16[64,256]{0,1:T(8,128)(2,1)S(1)}, u32[]{:S(2)}, u32[]{:S(2)}) collective-permute-start(bf16[64,256]{0,1:T(8,128)(2,1)S(1)} %collective-permute-done.3), channel_id=1, source_target_pairs={{0,256},{16,272},{32,288},{48,304},{64,320},{80,336},{96,352},{112... | collective-permute-start | bytes 98312 | tf_op jit(solution)/shard_map/ppermute | solution.py:20
  108.5 135.4 %all-gather.5.cloned.1.call-start = ((), (), s32[]{:S(2)}) async-start(), calls=%async_computation.4 | async-start | bytes 2162688 | tf_op jit(solution)/shard_map/all_gather | solution.py:111
  108.5 3.1 collective-permute-start.16
  111.6 5.8 collective-permute-start.17
  117.4 7.3 %collective-permute-start.18 = (bf16[64,256]{1,0:T(8,128)(2,1)S(1)}, bf16[64,256]{1,0:T(8,128)(2,1)S(1)}, u32[]{:S(2)}, u32[]{:S(2)}) collective-permute-start(bf16[64,256]{1,0:T(8,128)(2,1)S(1)} %collective-permute-done.17), channel_id=1, source_target_pairs={{0,64},{16,80},{32,96},{48,112},{64,0},{80,16},{96,32},{112,48},{1... | collective-permute-start | bytes 98312 | tf_op jit(solution)/shard_map/ppermute | solution.py:20
  124.7 5.8 collective-permute-start.19
  130.5 7.3 %collective-permute-start.20 = (bf16[64,256]{1,0:T(8,128)(2,1)S(1)}, bf16[64,256]{1,0:T(8,128)(2,1)S(1)}, u32[]{:S(2)}, u32[]{:S(2)}) collective-permute-start(bf16[64,256]{1,0:T(8,128)(2,1)S(1)} %collective-permute-done.19), channel_id=1, source_target_pairs={{0,256},{16,272},{32,288},{48,304},{64,320},{80,336},{96,352},{112... | collective-permute-start | bytes 98312 | tf_op jit(solution)/shard_map/ppermute | solution.py:20
  138.5 412.1 %reduce-scatter.4.cloned.1.call-start = ((), (), s32[]{:S(2)}) async-start(), calls=%async_computation.5 | async-start | bytes 2162688
  138.9 3.8 collective-permute-start.5
  142.7 16.7 %collective-permute-start.6 = (bf16[64,2048]{0,1:T(8,128)(2,1)S(1)}, bf16[64,2048]{0,1:T(8,128)(2,1)S(1)}, u32[]{:S(2)}, u32[]{:S(2)}) collective-permute-start(bf16[64,2048]{0,1:T(8,128)(2,1)S(1)} %collective-permute-done.5), channel_id=1, source_target_pairs={{0,32},{16,48},{32,0},{48,16},{64,96},{80,112},{96,64},{112,80},{1... | collective-permute-start | bytes 786440 | tf_op jit(solution)/shard_map/ppermute | solution.py:20
  159.4 17.6 %collective-permute-start.7 = (bf16[64,2048]{0,1:T(8,128)(2,1)S(1)}, bf16[64,2048]{0,1:T(8,128)(2,1)S(1)}, u32[]{:S(2)}, u32[]{:S(2)}) collective-permute-start(bf16[64,2048]{0,1:T(8,128)(2,1)S(1)} %collective-permute-done.6), channel_id=1, source_target_pairs={{0,64},{16,80},{32,96},{48,112},{64,0},{80,16},{96,32},{112,48},{1... | collective-permute-start | bytes 786440 | tf_op jit(solution)/shard_map/ppermute | solution.py:20
  177.0 14.7 %collective-permute-start.8 = (bf16[64,2048]{0,1:T(8,128)(2,1)S(1)}, bf16[64,2048]{0,1:T(8,128)(2,1)S(1)}, u32[]{:S(2)}, u32[]{:S(2)}) collective-permute-start(bf16[64,2048]{0,1:T(8,128)(2,1)S(1)} %collective-permute-done.7), channel_id=1, source_target_pairs={{0,128},{16,144},{32,160},{48,176},{64,192},{80,208},{96,224},{112... | collective-permute-start | bytes 786440 | tf_op jit(solution)/shard_map/ppermute | solution.py:20
  191.7 19.4 %collective-permute-start.9 = (bf16[64,2048]{0,1:T(8,128)(2,1)S(1)}, bf16[64,2048]{0,1:T(8,128)(2,1)S(1)}, u32[]{:S(2)}, u32[]{:S(2)}) collective-permute-start(bf16[64,2048]{0,1:T(8,128)(2,1)S(1)} %collective-permute-done.8), channel_id=1, source_target_pairs={{0,256},{16,272},{32,288},{48,304},{64,320},{80,336},{96,352},{112... | collective-permute-start | bytes 786440 | tf_op jit(solution)/shard_map/ppermute | solution.py:20
  197.7 3.1 collective-permute-start.11
  200.9 5.5 collective-permute-start.12
  206.3 7.0 %collective-permute-start.13 = (bf16[64,2]{0,1:T(2,128)(2,1)S(1)}, bf16[64,2]{0,1:T(2,128)(2,1)S(1)}, u32[]{:S(2)}, u32[]{:S(2)}) collective-permute-start(bf16[64,2]{0,1:T(2,128)(2,1)S(1)} %collective-permute-done.12), channel_id=1, source_target_pairs={{0,64},{16,80},{32,96},{48,112},{64,0},{80,16},{96,32},{112,48},{1... | collective-permute-start | bytes 776 | tf_op jit(solution)/shard_map/ppermute | solution.py:20
  213.3 5.8 collective-permute-start.14
  219.1 29.0 %collective-permute-start.15 = (bf16[64,2]{0,1:T(2,128)(2,1)S(1)}, bf16[64,2]{0,1:T(2,128)(2,1)S(1)}, u32[]{:S(2)}, u32[]{:S(2)}) collective-permute-start(bf16[64,2]{0,1:T(2,128)(2,1)S(1)} %collective-permute-done.14), channel_id=1, source_target_pairs={{0,256},{16,272},{32,288},{48,304},{64,320},{80,336},{96,352},{112... | collective-permute-start | bytes 776 | tf_op jit(solution)/shard_map/ppermute | solution.py:20
  403.0 3.4 collective-permute-start.21
  406.4 10.4 %collective-permute-start.22 = (bf16[64,2048]{1,0:T(8,128)(2,1)S(1)}, bf16[64,2048]{1,0:T(8,128)(2,1)S(1)}, u32[]{:S(2)}, u32[]{:S(2)}) collective-permute-start(bf16[64,2048]{1,0:T(8,128)(2,1)S(1)} %collective-permute-done.21), channel_id=1, source_target_pairs={{0,32},{16,48},{32,0},{48,16},{64,96},{80,112},{96,64},{112,80},{1... | collective-permute-start | bytes 786440 | tf_op jit(solution)/shard_map/ppermute | solution.py:20
  416.9 11.1 %collective-permute-start.23 = (bf16[64,2048]{1,0:T(8,128)(2,1)S(1)}, bf16[64,2048]{1,0:T(8,128)(2,1)S(1)}, u32[]{:S(2)}, u32[]{:S(2)}) collective-permute-start(bf16[64,2048]{1,0:T(8,128)(2,1)S(1)} %collective-permute-done.22), channel_id=1, source_target_pairs={{0,64},{16,80},{32,96},{48,112},{64,0},{80,16},{96,32},{112,48},{1... | collective-permute-start | bytes 786440 | tf_op jit(solution)/shard_map/ppermute | solution.py:20
  427.9 123.6 %collective-permute-start.24 = (bf16[64,2048]{1,0:T(8,128)(2,1)S(1)}, bf16[64,2048]{1,0:T(8,128)(2,1)S(1)}, u32[]{:S(2)}, u32[]{:S(2)}) collective-permute-start(bf16[64,2048]{1,0:T(8,128)(2,1)S(1)} %collective-permute-done.23), channel_id=1, source_target_pairs={{0,128},{16,144},{32,160},{48,176},{64,192},{80,208},{96,224},{112... | collective-permute-start | bytes 786440 | tf_op jit(solution)/shard_map/ppermute | solution.py:20
  551.5 33.1 %collective-permute-start.25 = (bf16[64,2048]{1,0:T(8,128)(2,1)S(1)}, bf16[64,2048]{1,0:T(8,128)(2,1)S(1)}, u32[]{:S(2)}, u32[]{:S(2)}) collective-permute-start(bf16[64,2048]{1,0:T(8,128)(2,1)S(1)} %collective-permute-done.24), channel_id=1, source_target_pairs={{0,256},{16,272},{32,288},{48,304},{64,320},{80,336},{96,352},{112... | collective-permute-start | bytes 786440 | tf_op jit(solution)/shard_map/ppermute | solution.py:20
  556.2 3.0 collective-permute-start.26
  559.2 5.5 collective-permute-start.27
  564.7 7.0 %collective-permute-start.28 = (bf16[64,2]{0,1:T(2,128)(2,1)S(1)}, bf16[64,2]{0,1:T(2,128)(2,1)S(1)}, u32[]{:S(2)}, u32[]{:S(2)}) collective-permute-start(bf16[64,2]{0,1:T(2,128)(2,1)S(1)} %collective-permute-done.27), channel_id=1, source_target_pairs={{0,64},{16,80},{32,96},{48,112},{64,0},{80,16},{96,32},{112,48},{1... | collective-permute-start | bytes 776 | tf_op jit(solution)/shard_map/ppermute | solution.py:20
  571.6 5.5 collective-permute-start.29
  577.1 7.0 %collective-permute-start.30 = (bf16[64,2]{0,1:T(2,128)(2,1)S(1)}, bf16[64,2]{0,1:T(2,128)(2,1)S(1)}, u32[]{:S(2)}, u32[]{:S(2)}) collective-permute-start(bf16[64,2]{0,1:T(2,128)(2,1)S(1)} %collective-permute-done.29), channel_id=1, source_target_pairs={{0,256},{16,272},{32,288},{48,304},{64,320},{80,336},{96,352},{112... | collective-permute-start | bytes 776 | tf_op jit(solution)/shard_map/ppermute | solution.py:20
Sparse Core Ops, SparseCore 0:
  76.3 64.1 all-reduce.1
Sparse Core Ops, SparseCore 1:
  108.5 70.2 all-gather.2
  181.8 61.9 all-gather.4
  448.0 102.6 reduce-scatter.3
